TPU v7x, 256 devices: a whole 4x4x8 slice. The times are simulated.
256 devices in a mesh: los: 16 (over x_lo, z), tile: 16 (over x_hi, y, core).
Axes of the slice: x: 4 (x_hi: 2, x_lo: 2; x = x_hi * 2 + x_lo), y: 4, z: 8, core: 2. Of those that a mesh axis runs over, the one named last changes fastest.
Arguments:
- density: bfloat16 [128, 512, 2048], P('tile', None, 'los'), may hold values from -18 to 18
- direction: bfloat16 [128, 512, 2048], P('tile', None, 'los'), may hold values from -6 to 6
- inverse_variance: bfloat16 [128, 512, 2048], P('tile', None, 'los'), may hold values from 0.25 to 4
- pixel_mask: int32 [128, 512, 2048], P('tile', None, 'los'), may hold values 0 or 1
- slot_count: int32 [16, 16], P('los', 'tile'), may hold values from 32 to 128, as said below
- slot_group: int32 [16, 16, 128], P('los', 'tile'), may hold values from 0 to 31
- slot_shift: int32 [16, 16, 128], P('los', 'tile'), may hold values from -1 to 1
- block_tiles: bfloat16 [16, 16, 128, 128, 128], P('los', 'tile'), as said below
Outputs:
- hessian_product: float32 [128, 512, 2048], P('tile', None, 'los')
Inputs may be any that keep to these rules, and one draw needn't show every extreme that they name: Only the first slot_count slots of a device's lists are used; the rest are ignored. `slot_shift`: A shift of -1 names the previous slab and 1 the next, wrapping around the sightline. `block_tiles`: entries are nonnegative.
All inputs are finite; a program needn't handle non-finite values. No bound on the sum of `pixel_mask` on one device may be relied on, other than what follows from the above.
Results may differ from a plain program's by a relative error of at most 0.0081.
Values may be sent and summed in bfloat16 or wider, within the bound.
A program may use at most 128 MiB of HBM per device.

v0:
```python
import jax
import jax.numpy as jnp
import numpy as np
from jax import lax
from jax.experimental import pallas as pl
from jax.experimental.pallas import tpu as pltpu
from jax.sharding import PartitionSpec as P

MESH = pl.DeviceIdType.MESH
GROUP = 128
SIGMA = 2
REACH = 6
ROWS = 8
WIDTH = 512
PIX = 128
SLOTS = 128
GROUPS = 32
PAD = 16
CUTS = (0, 128, 256, 384, 512)
SCALE = 2.0**-7
BF = jnp.bfloat16
F32 = jnp.float32


def taps():
    span = np.arange(-REACH, REACH + 1).astype(np.float32)
    values = np.exp(-span * span / np.float32(2.0 * SIGMA * SIGMA)).astype(np.float32)
    held = (values / values.sum(dtype=np.float32)).astype(BF).astype(np.float32)
    return [float(v) for v in held[REACH:]]


def smooth_rows_block(weights, get, put):
    rows = [get(r).astype(F32) for r in range(ROWS + 2 * REACH)]
    for a in range(ROWS):
        mid = a + REACH
        total = weights[0] * rows[mid]
        for k in range(1, REACH + 1):
            total = total + weights[k] * (rows[mid - k] + rows[mid + k])
        put(a, total.astype(BF))


def body(
    cuts,
    cnt_ref,
    grp_ref,
    shf_ref,
    den_ref,
    dir_ref,
    iv_ref,
    msk_ref,
    til_ref,
    out_ref,
    own,
    lo,
    hi,
    rs,
    kc,
    tau,
    mine,
    left,
    right,
    til,
    acc,
    wts,
    tabv,
    tabs,
    iv,
    msk,
    inner,
    send_l,
    send_r,
    got_l,
    got_r,
    pul,
    plo,
    phi,
    br,
    outv,
    load_sem,
    tab_sem,
    p1_send,
    p1_recv,
    p2_send,
    p2_recv,
    p4_send,
    p4_recv,
    p5_send,
    p5_recv,
    out_sem,
):
    n = len(cuts) - 1
    ycut = [0] + [z + PAD for z in cuts[1:-1]] + [WIDTH]
    vcut = [0] + [z - PAD for z in cuts[1:-1]] + [WIDTH]
    los, tile = lax.axis_index("los"), lax.axis_index("tile")
    n_los, n_tile = lax.axis_size("los"), lax.axis_size("tile")
    nxt = (lax.rem(los + 1, n_los), tile)
    prv = (lax.rem(los + n_los - 1, n_los), tile)
    up = (los, lax.rem(tile + 1, n_tile))
    down = (los, lax.rem(tile + n_tile - 1, n_tile))
    w = taps()

    barrier = pltpu.get_barrier_semaphore()
    for other in (nxt, prv, up, down):
        pl.semaphore_signal(barrier, inc=1, device_id=other, device_id_type=MESH)
    pl.semaphore_wait(barrier, 4)

    def remote(src, dst, send, recv, device):
        return pltpu.make_async_remote_copy(
            src_ref=src,
            dst_ref=dst,
            send_sem=send,
            recv_sem=recv,
            device_id=device,
            device_id_type=MESH,
        )

    p1 = []
    for c in range(n):
        ys = pl.ds(ycut[c], ycut[c + 1] - ycut[c])
        copies = []
        for f, src in enumerate((den_ref, dir_ref)):
            copies.append(
                remote(
                    src.at[pl.ds(ROWS - REACH, REACH), ys],
                    lo.at[f, :, ys],
                    p1_send.at[c, f, 0],
                    p1_recv.at[c, f, 0],
                    up,
                )
            )
            copies.append(
                remote(
                    src.at[pl.ds(0, REACH), ys],
                    hi.at[f, :, ys],
                    p1_send.at[c, f, 1],
                    p1_recv.at[c, f, 1],
                    down,
                )
            )
        for copy in copies:
            copy.start()
        p1.append(copies)
    loads = [
        pltpu.make_async_copy(den_ref, own.at[0], load_sem.at[0]),
        pltpu.make_async_copy(dir_ref, own.at[1], load_sem.at[1]),
        pltpu.make_async_copy(til_ref, til, load_sem.at[2]),
        pltpu.make_async_copy(iv_ref, iv, load_sem.at[3]),
        pltpu.make_async_copy(msk_ref, msk, load_sem.at[4]),
    ]
    for load in loads:
        load.start()

    lane = lax.broadcasted_iota(jnp.int32, (SLOTS, SLOTS), 1)
    sub = lax.broadcasted_iota(jnp.int32, (SLOTS, SLOTS), 0)
    count = cnt_ref[0, 0]
    key = (shf_ref[...] + 1) * GROUPS + grp_ref[...]
    key = jnp.where(lax.broadcasted_iota(jnp.int32, (1, SLOTS), 1) < count, key, -1)
    key_row = jnp.broadcast_to(key, (SLOTS, SLOTS))
    key_col = jnp.transpose(key_row)

    def highest(found):
        x = jnp.where(found, sub, -1)
        size = SLOTS
        while size > 8:
            size //= 2
            x = jnp.maximum(x[:size], x[size:])
        for shift in (4, 2, 1):
            x = jnp.maximum(x, pltpu.roll(x, shift, 0))
        return jnp.where(x < 0, SLOTS, x)

    tabv[0] = highest((key_col == key_row) & (sub < lane))
    tabv[1] = highest(key_col == lane)
    to_smem = pltpu.make_async_copy(tabv, tabs, tab_sem)
    to_smem.start()

    rows_i = lax.broadcasted_iota(jnp.int32, kc.shape, 0)
    cols_i = lax.broadcasted_iota(jnp.int32, kc.shape, 1)
    apart = jnp.abs(rows_i + PAD - cols_i)
    band = jnp.zeros(kc.shape, F32)
    for k in range(REACH + 1):
        band = jnp.where(apart == k, w[k], band)
    kc[...] = band.astype(BF)
    for a in range(ROWS):
        for edge in (0, PAD + WIDTH):
            for f in range(2):
                rs[f, a, pl.ds(edge, PAD)] = jnp.zeros((PAD, PIX), BF)
            br[a, pl.ds(edge, PAD)] = jnp.zeros((PAD, PIX), BF)

    loads[0].wait()
    loads[1].wait()

    p2 = []
    for c in range(n):
        for copy in p1[c]:
            copy.wait_recv()

        @pl.loop(0, (ycut[c + 1] - ycut[c]) // 16)
        def _(i, y0=ycut[c]):
            y = pl.multiple_of(y0 + i * 16, 16)
            for f in range(2):

                def get(r):
                    if r < REACH:
                        return lo[f, r, pl.ds(y, 16)]
                    if r < REACH + ROWS:
                        return own[f, r - REACH, pl.ds(y, 16)]
                    return hi[f, r - REACH - ROWS, pl.ds(y, 16)]

                def put(a, value):
                    rs[f, a, pl.ds(y + PAD, 16)] = value

                smooth_rows_block(w, get, put)

        z0, m = cuts[c], cuts[c + 1] - cuts[c]
        zs = pl.ds(z0, m)

        @pl.loop(0, ROWS)
        def _(a, z0=z0, m=m, zs=zs):
            both = jnp.concatenate(
                [rs[0, a, pl.ds(z0, m + 2 * PAD)], rs[1, a, pl.ds(z0, m + 2 * PAD)]], axis=1
            )
            su = jnp.dot(kc[:m, : m + 2 * PAD], both, preferred_element_type=F32)
            t = 0.5 * jnp.exp(1.6 * su[:, :PIX])
            tau[a, zs] = t
            mine[a, 0, zs] = t.astype(BF)
            mine[a, 1, zs] = (1.6 * t * su[:, PIX:]).astype(BF)

        copies = [
            remote(mine.at[:, :, zs], left.at[:, :, zs], p2_send.at[c, 0], p2_recv.at[c, 0], nxt),
            remote(mine.at[:, :, zs], right.at[:, :, zs], p2_send.at[c, 1], p2_recv.at[c, 1], prv),
        ]
        for copy in copies:
            copy.start()
        p2.append(copies)

    loads[2].wait()
    to_smem.wait()
    acc[SLOTS] = jnp.zeros((PIX, PIX), F32)

    @pl.loop(0, SLOTS)
    def _(q):
        acc[q] = til[q].astype(F32) * SCALE + acc[tabs[0, 0, q]]

    @pl.loop(0, 3 * GROUPS)
    def _(i):
        wts[i] = acc[tabs[1, 0, i]].astype(BF)

    loads[3].wait()
    loads[4].wait()

    p4 = []
    per_row = WIDTH // GROUP
    for c in range(n):
        for copy in p2[c]:
            copy.wait_recv()
        z0, m = cuts[c], cuts[c + 1] - cuts[c]
        zs = pl.ds(z0, m)

        @pl.loop(0, ROWS)
        def _(a, zs=zs, m=m, part=z0 // GROUP):
            g = a * per_row + part
            total = None
            for o, ref in enumerate((left, mine, right)):
                block = jnp.concatenate([ref[a, 0, zs], ref[a, 1, zs]], axis=0)
                term = jnp.dot(block, wts[o * GROUPS + g], preferred_element_type=F32)
                total = term if total is None else total + term
            total = total * (1.0 / SCALE)
            flux = jnp.exp(-total[:m])
            weight = msk[a, zs].astype(F32) * iv[a, zs].astype(F32)
            adjoint = (weight * flux * flux * total[m:]).astype(BF)
            back = [
                lax.dot_general(
                    adjoint,
                    wts[o * GROUPS + g],
                    (((1,), (1,)), ((), ())),
                    preferred_element_type=F32,
                )
                * (1.0 / SCALE)
                for o in range(3)
            ]
            send_l[a, zs] = back[0].astype(BF)
            inner[a, zs] = back[1]
            send_r[a, zs] = back[2].astype(BF)

        copies = [
            remote(send_r.at[:, zs], got_l.at[:, zs], p4_send.at[c, 0], p4_recv.at[c, 0], nxt),
            remote(send_l.at[:, zs], got_r.at[:, zs], p4_send.at[c, 1], p4_recv.at[c, 1], prv),
        ]
        for copy in copies:
            copy.start()
        p4.append(copies)

    p5 = []
    outs = []

    def finish(c):
        for copy in p5[c]:
            copy.wait_recv()

        @pl.loop(0, (cuts[c + 1] - cuts[c]) // 16)
        def _(i):
            y = pl.multiple_of(cuts[c] + i * 16, 16)

            def get(r):
                if r < REACH:
                    return plo[r, pl.ds(y, 16)]
                if r < REACH + ROWS:
                    return pul[r - REACH, pl.ds(y, 16)]
                return phi[r - REACH - ROWS, pl.ds(y, 16)]

            def put(a, value):
                br[a, pl.ds(y + PAD, 16)] = value

            smooth_rows_block(w, get, put)

        v0, m = vcut[c], vcut[c + 1] - vcut[c]

        @pl.loop(0, ROWS)
        def _(a):
            outv[a, pl.ds(v0, m)] = jnp.dot(
                kc[:m, : m + 2 * PAD], br[a, pl.ds(v0, m + 2 * PAD)], preferred_element_type=F32
            )

        copy = pltpu.make_async_copy(
            outv.at[:, pl.ds(v0, m)], out_ref.at[:, pl.ds(v0, m)], out_sem.at[c]
        )
        copy.start()
        outs.append(copy)

    for c in range(n):
        for copy in p4[c]:
            copy.wait_recv()
        zs = pl.ds(cuts[c], cuts[c + 1] - cuts[c])

        @pl.loop(0, ROWS)
        def _(a, zs=zs):
            real = inner[a, zs] + got_l[a, zs].astype(F32) + got_r[a, zs].astype(F32)
            pul[a, zs] = (1.6 * tau[a, zs] * real).astype(BF)

        copies = [
            remote(
                pul.at[pl.ds(ROWS - REACH, REACH), zs],
                plo.at[:, zs],
                p5_send.at[c, 0],
                p5_recv.at[c, 0],
                up,
            ),
            remote(
                pul.at[pl.ds(0, REACH), zs], phi.at[:, zs], p5_send.at[c, 1], p5_recv.at[c, 1], down
            ),
        ]
        for copy in copies:
            copy.start()
        p5.append(copies)
        if c:
            finish(c - 1)
    finish(n - 1)
    for group in (p1, p2, p4, p5):
        for copies in group:
            for copy in copies:
                copy.wait_send()
    for copy in outs:
        copy.wait()


def on_device(
    density,
    direction,
    inverse_variance,
    pixel_mask,
    slot_count,
    slot_group,
    slot_shift,
    block_tiles,
):
    cuts = CUTS
    n = len(cuts) - 1
    tallest = max([b - a for a, b in zip(cuts, cuts[1:])] + [WIDTH - cuts[-2] + PAD])
    any_spec = pl.BlockSpec(memory_space=pl.ANY)
    vmem = pl.BlockSpec(memory_space=pltpu.VMEM)
    dma = pltpu.SemaphoreType.DMA

    def kernel(*refs):
        body(cuts, *refs)

    return pl.pallas_call(
        kernel,
        name="hessian_product",
        out_shape=jax.ShapeDtypeStruct((ROWS, WIDTH, PIX), F32),
        in_specs=[
            pl.BlockSpec(memory_space=pltpu.SMEM),
            vmem,
            vmem,
            any_spec,
            any_spec,
            any_spec,
            any_spec,
            any_spec,
        ],
        out_specs=any_spec,
        scratch_shapes=[
            pltpu.VMEM((2, ROWS, WIDTH, PIX), BF),
            pltpu.VMEM((2, REACH, WIDTH, PIX), BF),
            pltpu.VMEM((2, REACH, WIDTH, PIX), BF),
            pltpu.VMEM((2, ROWS, WIDTH + 2 * PAD, PIX), BF),
            pltpu.VMEM((tallest, 256), BF),
            pltpu.VMEM((ROWS, WIDTH, PIX), F32),
            pltpu.VMEM((ROWS, 2, WIDTH, PIX), BF),
            pltpu.VMEM((ROWS, 2, WIDTH, PIX), BF),
            pltpu.VMEM((ROWS, 2, WIDTH, PIX), BF),
            pltpu.VMEM((SLOTS, PIX, PIX), BF),
            pltpu.VMEM((SLOTS + 1, PIX, PIX), F32),
            pltpu.VMEM((3 * GROUPS, PIX, PIX), BF),
            pltpu.VMEM((2, 8, SLOTS), jnp.int32),
            pltpu.SMEM((2, 8, SLOTS), jnp.int32),
            pltpu.VMEM((ROWS, WIDTH, PIX), BF),
            pltpu.VMEM((ROWS, WIDTH, PIX), jnp.int32),
            pltpu.VMEM((ROWS, WIDTH, PIX), F32),
            pltpu.VMEM((ROWS, WIDTH, PIX), BF),
            pltpu.VMEM((ROWS, WIDTH, PIX), BF),
            pltpu.VMEM((ROWS, WIDTH, PIX), BF),
            pltpu.VMEM((ROWS, WIDTH, PIX), BF),
            pltpu.VMEM((ROWS, WIDTH, PIX), BF),
            pltpu.VMEM((REACH, WIDTH, PIX), BF),
            pltpu.VMEM((REACH, WIDTH, PIX), BF),
            pltpu.VMEM((ROWS, WIDTH + 2 * PAD, PIX), BF),
            pltpu.VMEM((ROWS, WIDTH, PIX), F32),
            dma((5,)),
            dma,
            dma((n, 2, 2)),
            dma((n, 2, 2)),
            dma((n, 2)),
            dma((n, 2)),
            dma((n, 2)),
            dma((n, 2)),
            dma((n, 2)),
            dma((n, 2)),
            dma((n,)),
        ],
        compiler_params=pltpu.CompilerParams(
            collective_id=0, has_side_effects=True, vmem_limit_bytes=62 * 1024 * 1024
        ),
    )(
        slot_count,
        slot_group[0],
        slot_shift[0],
        density,
        direction,
        inverse_variance,
        pixel_mask,
        block_tiles[0, 0],
    )


def solution(mesh):
    placed = (
        P("tile", None, "los"),
        P("tile", None, "los"),
        P("tile", None, "los"),
        P("tile", None, "los"),
        P("los", "tile"),
        P("los", "tile", None),
        P("los", "tile", None),
        P("los", "tile", None, None, None),
    )
    return jax.shard_map(
        on_device, mesh=mesh, in_specs=placed, out_specs=P("tile", None, "los"), check_vma=False
    )
```

profile of v0, /device:TPU:31, one launch (start us, length us, event | category | flops | bytes accessed | tf_op | source)
XLA Modules:
  0.0 140.3 jit_solution(2490427067079477209)
XLA Ops:
  0.7 136.6 %hessian_product.1 = f32[8,512,128]{2,1,0:T(8,128)} custom-call(s32[1,1]{1,0:T(1,128)S(6)} %copy.10.refs_0_, s32[1,128]{1,0:T(1,128)} %bitcast.4, s32[1,128]{1,0:T(1,128)} %bitcast.5, bf16[8,512,128]{2,1,0:T(8,128)(2,1)} %refs_3_.1, bf16[8,512,128]{2,1,0:T(8,128)(2,1)} %refs_4_.1, bf16[8,512,128]{2,1,0:T(8,128)(2,1)} %refs_5_.1, s32[8,512,128]{2,1,0:T(8,128)} %refs_6_.1, ...), custom_call_target="tpu_custom_call" | custom-call | tf_op jit(solution)/shard_map/hessian_product/pallas_call | solution.py:386
  137.2 3.1 %copy.11 = f32[8,512,128]{2,1,0:T(8,128)} copy(f32[8,512,128]{2,1,0:T(8,128)} %hessian_product.1) | data formatting | bytes 4194304
where the time goes:
time: 140 us
  Pallas kernels  137 us (98%)
  local copies, waits for them, and re-layouts  3.06 us (2%)
    pallas_call x1, Pallas kernels, on_device(): pl.pallas_call(kernel, name='hessian_product', out_shape=jax.ShapeDtypeSt...  137 us
    unnamed x1, local copies, waits for them, and re-layouts  3.06 us

commit v1 on v0

--- a/solution.py
+++ b/solution.py
@@ -98,6 +98,10 @@
     up = (los, lax.rem(tile + 1, n_tile))
     down = (los, lax.rem(tile + n_tile - 1, n_tile))
     w = taps()
+    place = lax.rem(tile, 8)
+    shared = (place < 2) | (place > 5)
+    ends = lax.rem(los, 8)
+    late = (shared & (ends == 7), shared & (ends == 0))
 
     barrier = pltpu.get_barrier_semaphore()
     for other in (nxt, prv, up, down):
@@ -229,9 +233,12 @@
             remote(mine.at[:, :, zs], left.at[:, :, zs], p2_send.at[c, 0], p2_recv.at[c, 0], nxt),
             remote(mine.at[:, :, zs], right.at[:, :, zs], p2_send.at[c, 1], p2_recv.at[c, 1], prv),
         ]
-        for copy in copies:
-            copy.start()
+        for held, copy in zip(late, copies):
+            pl.when(jnp.logical_not(held))(copy.start)
         p2.append(copies)
+    for copies in p2:
+        for held, copy in zip(late, copies):
+            pl.when(held)(copy.start)
 
     loads[2].wait()
     to_smem.wait()

time: 140 us -> 120 us (0.86)
  Pallas kernels: 137 us -> 116 us
    pallas_call x1, Pallas kernels: 137 us -> 116 us  [on_device(): pl.pallas_call(kernel, name='hessian_product', out_shape=jax.ShapeDtypeSt...]
where the time goes in v1:
time: 120 us
  Pallas kernels  116 us (97%)
  local copies, waits for them, and re-layouts  3.06 us (3%)
    pallas_call x1, Pallas kernels, on_device(): pl.pallas_call(kernel, name='hessian_product', out_shape=jax.ShapeDtypeSt...  116 us
    unnamed x1, local copies, waits for them, and re-layouts  3.06 us

profile of v1, /device:TPU:31, one launch (start us, length us, event | category | flops | bytes accessed | tf_op | source)
XLA Modules:
  0.0 119.7 jit_solution(16121144126423087895)
XLA Ops:
  0.7 115.9 %hessian_product.1 = f32[8,512,128]{2,1,0:T(8,128)} custom-call(s32[1,1]{1,0:T(1,128)S(6)} %copy.10.refs_0_, s32[1,128]{1,0:T(1,128)} %bitcast.4, s32[1,128]{1,0:T(1,128)} %bitcast.5, bf16[8,512,128]{2,1,0:T(8,128)(2,1)} %refs_3_.1, bf16[8,512,128]{2,1,0:T(8,128)(2,1)} %refs_4_.1, bf16[8,512,128]{2,1,0:T(8,128)(2,1)} %refs_5_.1, s32[8,512,128]{2,1,0:T(8,128)} %refs_6_.1, ...), custom_call_target="tpu_custom_call" | custom-call | tf_op jit(solution)/shard_map/hessian_product/pallas_call | solution.py:393
  116.6 3.1 %copy.11 = f32[8,512,128]{2,1,0:T(8,128)} copy(f32[8,512,128]{2,1,0:T(8,128)} %hessian_product.1) | data formatting | bytes 4194304

commit v2 on v0

--- a/solution.py
+++ b/solution.py
@@ -18,6 +18,7 @@
 PAD = 16
 CUTS = (0, 128, 256, 384, 512)
 SCALE = 2.0**-7
+RELAYED = (0, 1)
 BF = jnp.bfloat16
 F32 = jnp.float32
 
@@ -87,6 +88,9 @@
     p5_send,
     p5_recv,
     out_sem,
+    rout,
+    hop_send,
+    hop_recv,
 ):
     n = len(cuts) - 1
     ycut = [0] + [z + PAD for z in cuts[1:-1]] + [WIDTH]
@@ -98,11 +102,35 @@
     up = (los, lax.rem(tile + 1, n_tile))
     down = (los, lax.rem(tile + n_tile - 1, n_tile))
     w = taps()
+    place, end = lax.rem(tile, n_tile // 2), lax.rem(los, n_los // 2)
+    shared = (place < 2) | (place > 5)
+    late = (shared & (end == n_los // 2 - 1), shared & (end == 0))
+    at_end = (end == n_los // 2 - 1) | (end == 0)
+    from_up, from_down = at_end & (place == 7), at_end & (place == 0)
+    relay_up, relay_down = at_end & (place == 5), at_end & (place == 2)
+
+    def across(step):
+        return (lax.rem(los + n_los // 2, n_los), lax.rem(tile + step, n_tile))
+
+    partners = (
+        (from_up, (6, 11)),
+        (from_down, (10, 5)),
+        (relay_up, (10, 11)),
+        (relay_down, (6, 5)),
+    )
 
     barrier = pltpu.get_barrier_semaphore()
     for other in (nxt, prv, up, down):
         pl.semaphore_signal(barrier, inc=1, device_id=other, device_id_type=MESH)
-    pl.semaphore_wait(barrier, 4)
+    for role, steps in partners:
+
+        @pl.when(role)
+        def _(steps=steps):
+            for step in steps:
+                pl.semaphore_signal(barrier, inc=1, device_id=across(step), device_id_type=MESH)
+
+    involved = from_up | from_down | relay_up | relay_down
+    pl.semaphore_wait(barrier, jnp.where(involved, 6, 4))
 
     def remote(src, dst, send, recv, device):
         return pltpu.make_async_remote_copy(
@@ -114,32 +142,51 @@
             device_id_type=MESH,
         )
 
+    high, low = pl.ds(ROWS - REACH, REACH), pl.ds(0, REACH)
+
+    def launch(role, direct, via):
+        if via is None:
+            direct.start()
+        else:
+            pl.when(role)(via.start)
+            pl.when(jnp.logical_not(role))(direct.start)
+
     p1 = []
     for c in range(n):
         ys = pl.ds(ycut[c], ycut[c + 1] - ycut[c])
         copies = []
         for f, src in enumerate((den_ref, dir_ref)):
-            copies.append(
-                remote(
-                    src.at[pl.ds(ROWS - REACH, REACH), ys],
-                    lo.at[f, :, ys],
-                    p1_send.at[c, f, 0],
-                    p1_recv.at[c, f, 0],
-                    up,
+            for d, (rows, dst, device) in enumerate(((high, lo, up), (low, hi, down))):
+                copies.append(
+                    remote(
+                        src.at[rows, ys],
+                        dst.at[f, :, ys],
+                        p1_send.at[c, f, d],
+                        p1_recv.at[c, f, d],
+                        device,
+                    )
                 )
-            )
-            copies.append(
-                remote(
-                    src.at[pl.ds(0, REACH), ys],
-                    hi.at[f, :, ys],
-                    p1_send.at[c, f, 1],
-                    p1_recv.at[c, f, 1],
-                    down,
-                )
-            )
         for copy in copies:
             copy.start()
         p1.append(copies)
+
+    def pass_on(arrivals, onward):
+        for role, copies in zip((relay_up, relay_down), onward):
+
+            @pl.when(role)
+            def _(copies=copies):
+                for arrival, copy in zip(arrivals, copies):
+                    arrival.wait_recv()
+                    copy.start()
+
+    def passed(arrivals, onward):
+        for role, copies in zip((relay_up, relay_down), onward):
+
+            @pl.when(role)
+            def _(copies=copies):
+                for copy in copies:
+                    copy.wait_send()
+
     loads = [
         pltpu.make_async_copy(den_ref, own.at[0], load_sem.at[0]),
         pltpu.make_async_copy(dir_ref, own.at[1], load_sem.at[1]),
@@ -193,6 +240,10 @@
     for c in range(n):
         for copy in p1[c]:
             copy.wait_recv()
+        if c == n - 1:
+            for copies in p2:
+                for held, copy in zip(late, copies):
+                    pl.when(held)(copy.start)
 
         @pl.loop(0, (ycut[c + 1] - ycut[c]) // 16)
         def _(i, y0=ycut[c]):
@@ -229,9 +280,12 @@
             remote(mine.at[:, :, zs], left.at[:, :, zs], p2_send.at[c, 0], p2_recv.at[c, 0], nxt),
             remote(mine.at[:, :, zs], right.at[:, :, zs], p2_send.at[c, 1], p2_recv.at[c, 1], prv),
         ]
-        for copy in copies:
-            copy.start()
         p2.append(copies)
+        for d, held in enumerate(late):
+            if c < n - 1:
+                pl.when(jnp.logical_not(held))(copies[d].start)
+            else:
+                copies[d].start()
 
     loads[2].wait()
     to_smem.wait()
@@ -292,6 +346,7 @@
 
     p5 = []
     outs = []
+    back = []
 
     def finish(c):
         for copy in p5[c]:
@@ -337,28 +392,35 @@
             real = inner[a, zs] + got_l[a, zs].astype(F32) + got_r[a, zs].astype(F32)
             pul[a, zs] = (1.6 * tau[a, zs] * real).astype(BF)
 
-        copies = [
-            remote(
-                pul.at[pl.ds(ROWS - REACH, REACH), zs],
-                plo.at[:, zs],
-                p5_send.at[c, 0],
-                p5_recv.at[c, 0],
-                up,
-            ),
-            remote(
-                pul.at[pl.ds(0, REACH), zs], phi.at[:, zs], p5_send.at[c, 1], p5_recv.at[c, 1], down
-            ),
-        ]
-        for copy in copies:
-            copy.start()
+        copies, arrivals, onward = [], [], ([], [])
+        for d, (rows, dst, device, role, step) in enumerate(
+            ((high, plo, up, from_up, 6), (low, phi, down, from_down, 10))
+        ):
+            sems = (p5_send.at[c, d], p5_recv.at[c, d])
+            direct = remote(pul.at[rows, zs], dst.at[:, zs], *sems, device)
+            via = None
+            if c in RELAYED:
+                kept = rout.at[:, zs]
+                via = remote(pul.at[rows, zs], kept, sems[0], hop_recv.at[c], across(step))
+                goal = across((11, 5)[d])
+                onward[d].append(remote(kept, dst.at[:, zs], hop_send.at[c], sems[1], goal))
+                if d == 0:
+                    arrivals.append(via)
+            launch(role, direct, via)
+            copies.append(direct)
         p5.append(copies)
-        if c:
-            finish(c - 1)
-    finish(n - 1)
+        if arrivals:
+            back.append((arrivals, onward))
+    for relayed in back:
+        pass_on(*relayed)
+    for c in range(n):
+        finish(c)
     for group in (p1, p2, p4, p5):
         for copies in group:
             for copy in copies:
                 copy.wait_send()
+    for relayed in back:
+        passed(*relayed)
     for copy in outs:
         copy.wait()
 
@@ -436,6 +498,9 @@
             dma((n, 2)),
             dma((n, 2)),
             dma((n,)),
+            pltpu.VMEM((REACH, WIDTH, PIX), BF),
+            dma((n,)),
+            dma((n,)),
         ],
         compiler_params=pltpu.CompilerParams(
             collective_id=0, has_side_effects=True, vmem_limit_bytes=62 * 1024 * 1024

time: 140 us -> 112 us (0.80)
  Pallas kernels: 137 us -> 108 us
    pallas_call x1, Pallas kernels: 137 us -> 108 us  [on_device(): pl.pallas_call(kernel, name='hessian_product', out_shape=jax.ShapeDtypeSt...]
where the time goes in v2:
time: 112 us; the launch traced here: 111 us
  Pallas kernels  108 us (96%)
  local copies, waits for them, and re-layouts  3.06 us (3%)
    pallas_call x1, Pallas kernels, on_device(): pl.pallas_call(kernel, name='hessian_product', out_shape=jax.ShapeDtypeSt...  108 us
    unnamed x1, local copies, waits for them, and re-layouts  3.06 us

profile of v2, /device:TPU:31, one launch (start us, length us, event | category | flops | bytes accessed | tf_op | source)
XLA Modules:
  0.0 111.3 jit_solution(1590093591786256174)
XLA Ops:
  0.7 107.6 %hessian_product.1 = f32[8,512,128]{2,1,0:T(8,128)} custom-call(s32[1,1]{1,0:T(1,128)S(6)} %copy.10.refs_0_, s32[1,128]{1,0:T(1,128)} %bitcast.4, s32[1,128]{1,0:T(1,128)} %bitcast.5, bf16[8,512,128]{2,1,0:T(8,128)(2,1)} %refs_3_.1, bf16[8,512,128]{2,1,0:T(8,128)(2,1)} %refs_4_.1, bf16[8,512,128]{2,1,0:T(8,128)(2,1)} %refs_5_.1, s32[8,512,128]{2,1,0:T(8,128)} %refs_6_.1, ...), custom_call_target="tpu_custom_call" | custom-call | tf_op jit(solution)/shard_map/hessian_product/pallas_call | solution.py:448
  108.3 3.1 %copy.11 = f32[8,512,128]{2,1,0:T(8,128)} copy(f32[8,512,128]{2,1,0:T(8,128)} %hessian_product.1) | data formatting | bytes 4194304

commit v3 on v2

--- a/solution.py
+++ b/solution.py
@@ -18,7 +18,8 @@
 PAD = 16
 CUTS = (0, 128, 256, 384, 512)
 SCALE = 2.0**-7
-RELAYED = (0, 1)
+RELAYED = (0,)
+TURNED = (2,)
 BF = jnp.bfloat16
 F32 = jnp.float32
 
@@ -91,6 +92,9 @@
     rout,
     hop_send,
     hop_recv,
+    side,
+    side_send,
+    side_recv,
 ):
     n = len(cuts) - 1
     ycut = [0] + [z + PAD for z in cuts[1:-1]] + [WIDTH]
@@ -119,7 +123,18 @@
         (relay_down, (6, 5)),
     )
 
+    middle = jnp.logical_not(shared)
+    turn = (middle & (end == n_los // 2 - 1), middle & (end == 0))
+    over = jnp.where(end == 0, prv[0], nxt[0])
+    beside = lax.rem(tile + jnp.where((place < 2) | (place == 4) | (place == 5), 2, 14), n_tile)
+
     barrier = pltpu.get_barrier_semaphore()
+
+    @pl.when(at_end)
+    def _():
+        for other in ((los, beside), (over, beside)):
+            pl.semaphore_signal(barrier, inc=1, device_id=other, device_id_type=MESH)
+
     for other in (nxt, prv, up, down):
         pl.semaphore_signal(barrier, inc=1, device_id=other, device_id_type=MESH)
     for role, steps in partners:
@@ -130,7 +145,7 @@
                 pl.semaphore_signal(barrier, inc=1, device_id=across(step), device_id_type=MESH)
 
     involved = from_up | from_down | relay_up | relay_down
-    pl.semaphore_wait(barrier, jnp.where(involved, 6, 4))
+    pl.semaphore_wait(barrier, jnp.where(involved, 6, 4) + jnp.where(at_end, 2, 0))
 
     def remote(src, dst, send, recv, device):
         return pltpu.make_async_remote_copy(
@@ -302,7 +317,7 @@
     loads[3].wait()
     loads[4].wait()
 
-    p4 = []
+    p4, turned = [], []
     per_row = WIDTH // GROUP
     for c in range(n):
         for copy in p2[c]:
@@ -336,13 +351,26 @@
             inner[a, zs] = back[1]
             send_r[a, zs] = back[2].astype(BF)
 
-        copies = [
-            remote(send_r.at[:, zs], got_l.at[:, zs], p4_send.at[c, 0], p4_recv.at[c, 0], nxt),
-            remote(send_l.at[:, zs], got_r.at[:, zs], p4_send.at[c, 1], p4_recv.at[c, 1], prv),
-        ]
-        for copy in copies:
-            copy.start()
+        copies = []
+        for d, (src, dst, device) in enumerate(((send_r, got_l, nxt), (send_l, got_r, prv))):
+            sems = (p4_send.at[c, d], p4_recv.at[c, d])
+            direct = remote(src.at[:, zs], dst.at[:, zs], *sems, device)
+            via = None
+            if c in TURNED:
+                kept = side.at[:, zs]
+                via = remote(src.at[:, zs], kept, sems[0], side_recv.at[c], (los, beside))
+                on = remote(kept, dst.at[:, zs], side_send.at[c], sems[1], (over, beside))
+                turned.append((turn[d], via, on))
+            launch(late[d], direct, via)
+            copies.append(direct)
         p4.append(copies)
+
+    for role, via, on in turned:
+
+        @pl.when(role)
+        def _(via=via, on=on):
+            via.wait_recv()
+            on.start()
 
     p5 = []
     outs = []
@@ -421,6 +449,8 @@
                 copy.wait_send()
     for relayed in back:
         passed(*relayed)
+    for role, _, on in turned:
+        pl.when(role)(on.wait_send)
     for copy in outs:
         copy.wait()
 
@@ -501,6 +531,9 @@
             pltpu.VMEM((REACH, WIDTH, PIX), BF),
             dma((n,)),
             dma((n,)),
+            pltpu.VMEM((ROWS, WIDTH, PIX), BF),
+            dma((n,)),
+            dma((n,)),
         ],
         compiler_params=pltpu.CompilerParams(
             collective_id=0, has_side_effects=True, vmem_limit_bytes=62 * 1024 * 1024

time: 112 us -> 111 us (level)
  Pallas kernels: 108 us -> 106 us
    pallas_call x1, Pallas kernels: 108 us -> 106 us  [on_device(): pl.pallas_call(kernel, name='hessian_product', out_shape=jax.ShapeDtypeSt...]
where the time goes in v3:
time: 111 us; the launch traced here: 109 us
  Pallas kernels  106 us (95%)
  local copies, waits for them, and re-layouts  3.06 us (3%)
    pallas_call x1, Pallas kernels, on_device(): pl.pallas_call(kernel, name='hessian_product', out_shape=jax.ShapeDtypeSt...  106 us
    unnamed x1, local copies, waits for them, and re-layouts  3.06 us

profile of v3, /device:TPU:31, one launch (start us, length us, event | category | flops | bytes accessed | tf_op | source)
XLA Modules:
  0.0 109.2 jit_solution(16778201733231848319)
XLA Ops:
  0.7 105.5 %hessian_product.1 = f32[8,512,128]{2,1,0:T(8,128)} custom-call(s32[1,1]{1,0:T(1,128)S(6)} %copy.10.refs_0_, s32[1,128]{1,0:T(1,128)} %bitcast.4, s32[1,128]{1,0:T(1,128)} %bitcast.5, bf16[8,512,128]{2,1,0:T(8,128)(2,1)} %refs_3_.1, bf16[8,512,128]{2,1,0:T(8,128)(2,1)} %refs_4_.1, bf16[8,512,128]{2,1,0:T(8,128)(2,1)} %refs_5_.1, s32[8,512,128]{2,1,0:T(8,128)} %refs_6_.1, ...), custom_call_target="tpu_custom_call" | custom-call | tf_op jit(solution)/shard_map/hessian_product/pallas_call | solution.py:478
  106.2 3.1 %copy.11 = f32[8,512,128]{2,1,0:T(8,128)} copy(f32[8,512,128]{2,1,0:T(8,128)} %hessian_product.1) | data formatting | bytes 4194304
